TPU v7x, 128 devices: a whole 4x4x4 slice. The times are simulated.
128 devices in a mesh: row: 8 (over z, core), col: 16 (over x, y).
Axes of the slice: x: 4, y: 4, z: 4, core: 2. Of those that a mesh axis runs over, the one named last changes fastest.
Arguments:
- embed: bfloat16 [262144, 64], P(('row', 'col')), may hold values from -6 to 6
- tiles: bfloat16 [8192, 128, 128], P(('row', 'col'))
- tile_rows: int32 [8192], P(('row', 'col')), may hold values from 0 to 2047, as said below
- tile_cols: int32 [8192], P(('row', 'col')), may hold values from 0 to 2047, as said below
- chg_tiles: bfloat16 [24576, 128, 128], P(('row', 'col'))
- chg_rows: int32 [24576], P(('row', 'col')), may hold values from 0 to 2047, as said below
- chg_cols: int32 [24576], P(('row', 'col')), may hold values from 0 to 2047, as said below
Outputs:
- embedding: float32 [262144, 64], P(('row', 'col'))
Inputs may be any that keep to these rules, and one draw needn't show every extreme that they name: Tile n lies in the row group of the device that holds it: tile_rows[n] // 256 equals (n // 64) // 16. Tile n lies in the column group of the device that holds it: tile_cols[n] // 128 equals (n // 64) % 16. `chg_rows`: one device's list names each transpose owner at most 3 times; in every draw some owner is named exactly 3 times by every device's list. `chg_cols`: read with chg_rows to give the transpose owner.
All inputs are finite; a program needn't handle non-finite values.
Results may differ from a plain program's by a relative error of at most 0.025.
Values may be sent and summed in bfloat16 or wider, within the bound.
A program may use at most 192 MiB of HBM per device.

v0:
```python
import jax
import jax.numpy as jnp
from jax import lax
from jax.sharding import PartitionSpec as P

ITERS = 3
CAP = 3


def block_terms(own, own_rows, own_cols, taken, taken_rows, taken_cols, blocked, row_blocks):
    own_terms = jnp.einsum(
        "nab,nbk->nak", own, blocked[own_cols], preferred_element_type=jnp.float32
    )
    taken_terms = jnp.einsum(
        "nab,nak->nbk", taken, blocked[taken_cols], preferred_element_type=jnp.float32
    )
    return jax.ops.segment_sum(own_terms, own_rows, row_blocks) + jax.ops.segment_sum(
        taken_terms, taken_rows, row_blocks
    )


def local(embed, tiles, tile_rows, tile_cols, chg_tiles, chg_rows, chg_cols):
    rows_dev, feature_width = embed.shape
    tile_size = tiles.shape[1]
    row_count = lax.axis_size("row")
    col_count = lax.axis_size("col")
    devices = row_count * col_count
    row_blocks = rows_dev * col_count // tile_size
    col_blocks = rows_dev * row_count // tile_size
    sub_rows = rows_dev // devices
    owners = chg_cols // row_blocks * col_count + chg_rows // col_blocks
    position = jnp.arange(owners.shape[0], dtype=jnp.int32)
    earlier = position[None, :] < position[:, None]
    slot_rank = jnp.sum(jnp.logical_and(owners[:, None] == owners[None, :], earlier), axis=1)
    outgoing = (
        jnp.zeros((devices, CAP, tile_size, tile_size), jnp.bfloat16)
        .at[owners, slot_rank]
        .set(chg_tiles)
    )
    placing = jnp.stack([chg_cols % row_blocks, chg_rows % col_blocks], axis=1)
    output_slots = jnp.zeros((devices, CAP, 2), jnp.int32).at[owners, slot_rank].set(placing)
    taken, taken_places = (
        lax.all_to_all(outgoing, ("row", "col"), split_axis=0, concat_axis=0, tiled=True),
        lax.all_to_all(output_slots, ("row", "col"), split_axis=0, concat_axis=0, tiled=True),
    )
    taken = taken.reshape(devices * CAP, tile_size, tile_size)
    taken_places = taken_places.reshape(devices * CAP, 2)
    taken_rows = taken_places[:, 0]
    taken_cols = taken_places[:, 1]
    own_rows = tile_rows % row_blocks
    own_cols = tile_cols % col_blocks
    degree_terms = jax.ops.segment_sum(
        jnp.sum(jnp.abs(tiles), axis=2, dtype=jnp.float32), own_rows, row_blocks
    )
    degree_terms = degree_terms + jax.ops.segment_sum(
        jnp.sum(jnp.abs(taken), axis=1, dtype=jnp.float32), taken_rows, row_blocks
    )
    degree = 1.0 + lax.psum_scatter(
        degree_terms.astype(jnp.bfloat16), "col", scatter_dimension=0, tiled=True
    ).astype(jnp.float32).reshape(rows_dev, 1)
    nodes = rows_dev * devices
    current = embed
    final_output = embed.astype(jnp.float32)
    for iteration in range(ITERS):
        received_terms = lax.all_to_all(
            current.reshape(devices, sub_rows, feature_width),
            ("row", "col"),
            split_axis=0,
            concat_axis=0,
            tiled=True,
        )
        group = lax.all_gather(
            received_terms.reshape(rows_dev, feature_width), "row", axis=0, tiled=True
        )
        blocked = group.reshape(col_blocks, tile_size, feature_width)
        partial_value = block_terms(
            tiles, own_rows, own_cols, taken, taken_rows, taken_cols, blocked, row_blocks
        )
        summed = lax.psum_scatter(
            partial_value.reshape(row_blocks * tile_size, feature_width).astype(jnp.bfloat16),
            "col",
            scatter_dimension=0,
            tiled=True,
        ).astype(jnp.float32)
        scaled = summed / degree
        local_gram = jnp.dot(
            scaled.T, scaled, precision=lax.Precision.HIGHEST, preferred_element_type=jnp.float32
        )
        gram = lax.psum(local_gram, ("row", "col")) / nodes
        lower = jnp.linalg.cholesky(gram)
        final_output = lax.linalg.triangular_solve(
            lower, scaled, left_side=False, lower=True, transpose_a=True
        )
        current = final_output.astype(jnp.bfloat16)
    return final_output


def solution(mesh):
    placed = (
        P(("row", "col"), None),
        P(("row", "col"), None, None),
        P(("row", "col")),
        P(("row", "col")),
        P(("row", "col"), None, None),
        P(("row", "col")),
        P(("row", "col")),
    )
    return jax.shard_map(
        local, mesh=mesh, in_specs=placed, out_specs=P(("row", "col"), None), check_vma=False
    )
```

profile of v0, /device:TPU:1, one launch (start us, length us, event | category | flops | bytes accessed | tf_op | source)
XLA Modules:
  0.0 1204.5 jit_solution(14980614209809009102)
XLA Ops:
  8.4 10.1 scatter_fusion.1
  20.0 11.5 all-to-all-start.1
  33.8 7.8 all-to-all-done.1
  41.6 4.1 all-to-all-start
  45.7 7.7 broadcast_in_dim.14
  53.4 30.8 %scatter_fusion.2 = bf16[128,3,128,128]{3,2,1,0:T(8,128)(2,1)} fusion(bf16[128,3,128,128]{3,2,1,0:T(8,128)(2,1)} %broadcast_in_dim.14, s32[192]{0:T(256)S(1)} %bitcast.91, bf16[192,128,128]{2,1,0:T(8,128)(2,1)} %param.14), kind=kCustom, calls=%fused_computation.8 | custom fusion | bytes 18875904 | tf_op jit(solution)/shard_map/scatter | solution.py:38
  84.2 10.2 all-to-all-start.2
  97.6 142.3 %all-gather.4.cloned.1.call-done = bf16[16384,64]{1,0:T(8,128)(2,1)} async-done(((bf16[2048,64]{1,0:T(8,128)(2,1)}), bf16[16384,64]{1,0:T(8,128)(2,1)}) %all-gather.4.cloned.1.call-update) | async-done | bytes 2097168 | tf_op jit(solution)/shard_map/all_gather | solution.py:72
  239.9 3.9 copy.77
  243.8 13.3 %gather_fusion.1 = bf16[384,128,64]{1,2,0:T(8,128)(2,1)} fusion(bf16[128,128,64]{1,2,0:T(8,128)(2,1)S(1)} %copy.77, s32[1024]{0:T(1024)S(1)} %pad_clamp_fusion), kind=kCustom, calls=%fused_computation.1 | custom fusion | bytes 12584448 | tf_op jit(solution)/shard_map/gather | solution.py:15
  260.9 4.3 broadcast.110.clone.2
  265.2 9.0 scatter_fusion
  274.2 9.2 convert_reduce_fusion
  286.7 14.3 %fusion.38 = f32[384,128,64]{1,2,0:T(8,128)} fusion(bf16[384,128,64]{1,2,0:T(8,128)(2,1)} %gather_fusion.1, bf16[384,128,128]{2,1,0:T(8,128)(2,1)} %bitcast.9), kind=kOutput, calls=%fused_computation.120 | convolution fusion | flops 805306368 | bytes 31457280 | tf_op jit(solution)/shard_map/nab,nak->nbk/dot_general | solution.py:14
  301.0 4.3 broadcast.110.clone.3
  305.3 59.8 %scatter_fusion.3 = f32[256,128,64]{1,2,0:T(8,128)} fusion(f32[256,128,64]{1,2,0:T(8,128)} %broadcast.110.clone.3, s32[384]{0:T(512)S(1)} %get-tuple-element.8, f32[384,128,64]{1,2,0:T(8,128)} %fusion.38), kind=kCustom, calls=%fused_computation.9 | custom fusion | flops 3145728 | bytes 37750272 | tf_op jit(solution)/shard_map/scatter-add | solution.py:17
  365.1 8.6 copy_bitcast_fusion.2
  375.0 8.3 all-reduce.3.cloned.1.call-done
  384.0 84.0 %reduce-scatter.4.cloned.1.call-done = bf16[2048,64]{0,1:T(8,128)(2,1)} async-done(((bf16[32768,64]{0,1:T(8,128)(2,1)}), bf16[2048,64]{0,1:T(8,128)(2,1)}) %reduce-scatter.4.cloned.1.call-update) | async-done | bytes 262160 | tf_op jit(solution)/shard_map/reduce_scatter | solution.py:79
  469.7 66.1 %psum.21 = f32[64,64]{0,1:T(8,128)S(1)} all-reduce(f32[64,64]{0,1:T(8,128)S(1)} %fusion.5), channel_id=1, replica_groups=mesh['row'=8,'col'=16] {'row','col'}, use_global_device_ids=true, to_apply=%region_11.12 | all-reduce | flops 4096 | bytes 32768 | tf_op jit(solution)/shard_map/psum | solution.py:89
  535.9 5.8 cholesky.59
  543.1 4.9 custom-call.11
  550.2 15.7 %all_to_all.25 = bf16[128,2,512]{2,1,0:T(2,128)(2,1)S(1)} all-to-all(bf16[128,2,512]{2,1,0:T(2,128)(2,1)S(1)} %reshape.237), channel_id=1, replica_groups=mesh['row'=8,'col'=16] {'row','col'}, dimensions={0} | all-to-all | bytes 524288 | tf_op jit(solution)/shard_map/all_to_all | solution.py:65
  567.3 28.7 %all-gather.6.cloned.1.call-done = bf16[16384,64]{1,0:T(8,128)(2,1)} async-done(((bf16[2048,64]{1,0:T(8,128)(2,1)}), bf16[16384,64]{1,0:T(8,128)(2,1)}) %all-gather.6.cloned.1.call-update) | async-done | bytes 2097168 | tf_op jit(solution)/shard_map/all_gather | solution.py:72
  599.6 13.3 %gather_fusion.3 = bf16[384,128,64]{1,2,0:T(8,128)(2,1)} fusion(bf16[128,128,64]{1,2,0:T(8,128)(2,1)S(1)} %copy.87, s32[1024]{0:T(1024)S(1)} %pad_clamp_fusion), kind=kCustom, calls=%fused_computation.3 | custom fusion | bytes 12584448 | tf_op jit(solution)/shard_map/gather | solution.py:15
  613.7 14.4 %fusion.39 = f32[384,128,64]{1,2,0:T(8,128)} fusion(bf16[384,128,64]{1,2,0:T(8,128)(2,1)} %gather_fusion.3, bf16[384,128,128]{2,1,0:T(8,128)(2,1)} %bitcast.9), kind=kOutput, calls=%fused_computation.121 | convolution fusion | flops 805306368 | bytes 31457280 | tf_op jit(solution)/shard_map/nab,nak->nbk/dot_general | solution.py:14
  629.6 4.3 broadcast.110.clone.4
  633.9 59.8 %scatter_fusion.5 = f32[256,128,64]{1,2,0:T(8,128)} fusion(f32[256,128,64]{1,2,0:T(8,128)} %broadcast.110.clone.4, s32[384]{0:T(512)S(1)} %get-tuple-element.8, f32[384,128,64]{1,2,0:T(8,128)} %fusion.39), kind=kCustom, calls=%fused_computation.13 | custom fusion | flops 3145728 | bytes 37750272 | tf_op jit(solution)/shard_map/scatter-add | solution.py:17
  693.7 4.3 broadcast.110.clone.1
  698.0 9.2 scatter_fusion.4
  707.2 8.6 copy_bitcast_fusion.1
  715.9 75.9 %reduce-scatter.6.cloned.1.call-done = bf16[2048,64]{0,1:T(8,128)(2,1)} async-done(((bf16[32768,64]{0,1:T(8,128)(2,1)}), bf16[2048,64]{0,1:T(8,128)(2,1)}) %reduce-scatter.6.cloned.1.call-update) | async-done | bytes 262160 | tf_op jit(solution)/shard_map/reduce_scatter | solution.py:79
  793.4 66.2 %psum.22 = f32[64,64]{0,1:T(8,128)S(1)} all-reduce(f32[64,64]{0,1:T(8,128)S(1)} %fusion.6), channel_id=1, replica_groups=mesh['row'=8,'col'=16] {'row','col'}, use_global_device_ids=true, to_apply=%region_17.20 | all-reduce | flops 4096 | bytes 32768 | tf_op jit(solution)/shard_map/psum | solution.py:89
  859.7 5.8 cholesky.70
  866.9 4.9 custom-call.12
  873.9 15.7 %all_to_all.26 = bf16[128,2,512]{2,1,0:T(2,128)(2,1)S(1)} all-to-all(bf16[128,2,512]{2,1,0:T(2,128)(2,1)S(1)} %reshape.239), channel_id=1, replica_groups=mesh['row'=8,'col'=16] {'row','col'}, dimensions={0} | all-to-all | bytes 524288 | tf_op jit(solution)/shard_map/all_to_all | solution.py:65
  890.9 28.8 %all-gather.8.cloned.1.call-done = bf16[16384,64]{1,0:T(8,128)(2,1)} async-done(((bf16[2048,64]{1,0:T(8,128)(2,1)}), bf16[16384,64]{1,0:T(8,128)(2,1)}) %all-gather.8.cloned.1.call-update) | async-done | bytes 2097168 | tf_op jit(solution)/shard_map/all_gather | solution.py:72
  923.4 13.3 %gather_fusion.5 = bf16[384,128,64]{1,2,0:T(8,128)(2,1)} fusion(bf16[128,128,64]{1,2,0:T(8,128)(2,1)S(1)} %copy.94, s32[1024]{0:T(1024)S(1)} %pad_clamp_fusion), kind=kCustom, calls=%fused_computation.5 | custom fusion | bytes 12584448 | tf_op jit(solution)/shard_map/gather | solution.py:15
  937.5 14.4 %fusion.40 = f32[384,128,64]{1,2,0:T(8,128)} fusion(bf16[384,128,64]{1,2,0:T(8,128)(2,1)} %gather_fusion.5, bf16[384,128,128]{2,1,0:T(8,128)(2,1)} %bitcast.9), kind=kOutput, calls=%fused_computation.122 | convolution fusion | flops 805306368 | bytes 31457280 | tf_op jit(solution)/shard_map/nab,nak->nbk/dot_general | solution.py:14
  953.4 4.3 broadcast.110.clone.5
  957.7 58.9 %scatter_fusion.7 = f32[256,128,64]{1,2,0:T(8,128)} fusion(f32[256,128,64]{1,2,0:T(8,128)} %broadcast.110.clone.5, s32[384]{0:T(512)S(1)} %get-tuple-element.8, f32[384,128,64]{1,2,0:T(8,128)} %fusion.40), kind=kCustom, calls=%fused_computation.15 | custom fusion | flops 3145728 | bytes 37750272 | tf_op jit(solution)/shard_map/scatter-add | solution.py:17
  1016.6 4.3 broadcast.110.clone
  1020.9 9.2 scatter_fusion.6
  1030.1 8.5 copy_bitcast_fusion
  1038.7 75.5 %reduce-scatter.8.cloned.1.call-done = bf16[2048,64]{0,1:T(8,128)(2,1)} async-done(((bf16[32768,64]{0,1:T(8,128)(2,1)}), bf16[2048,64]{0,1:T(8,128)(2,1)}) %reduce-scatter.8.cloned.1.call-update) | async-done | bytes 262160 | tf_op jit(solution)/shard_map/reduce_scatter | solution.py:79
  1115.9 66.3 %psum.23 = f32[64,64]{0,1:T(8,128)S(1)} all-reduce(f32[64,64]{0,1:T(8,128)S(1)} %fusion.7), channel_id=1, replica_groups=mesh['row'=8,'col'=16] {'row','col'}, use_global_device_ids=true, to_apply=%region_21.24 | all-reduce | flops 4096 | bytes 32768 | tf_op jit(solution)/shard_map/psum | solution.py:89
  1182.2 5.8 cholesky.81
  1189.4 4.9 custom-call.13
  (90 shorter events, 46.8 us)
Async XLA Ops:
  20.0 21.6 %all-to-all-start.1 = ((s32[128,3,2]{1,2,0:T(2,128)}), s32[128,3,2]{1,2,0:T(2,128)S(1)}, u32[]{:S(2)}, u32[]{:S(2)}) async-start(s32[128,3,2]{1,2,0:T(2,128)} %copy.79), calls=%async_computation.1 | async-start | bytes 262144 | tf_op jit(solution)/shard_map/all_to_all | solution.py:44
  41.6 42.6 %all-to-all-start = ((bf16[128,2,512]{2,1,0:T(2,128)(2,1)}), bf16[128,2,512]{2,1,0:T(2,128)(2,1)S(1)}, u32[]{:S(2)}, u32[]{:S(2)}) async-start(bf16[128,2,512]{2,1,0:T(2,128)(2,1)} %reshape.235), calls=%async_computation | async-start | bytes 524288 | tf_op jit(solution)/shard_map/all_to_all | solution.py:65
  84.2 11.5 copy-start.3
  84.2 11.6 copy-start
  84.2 13.1 %copy-start.4 = (s32[64]{0:T(128)S(1)}, s32[64]{0:T(128)}, u32[]{:S(2)}) copy-start(s32[64]{0:T(128)} %param.13) | copy-start | bytes 772
  84.2 190.0 %all-to-all-start.2 = ((bf16[128,3,128,128]{3,2,1,0:T(8,128)(2,1)}), bf16[128,3,128,128]{3,2,1,0:T(8,128)(2,1)}, u32[]{:S(2)}, u32[]{:S(2)}) async-start(bf16[128,3,128,128]{3,2,1,0:T(8,128)(2,1)} %scatter_fusion.2), calls=%async_computation.2 | async-start | bytes 25165824 | tf_op jit(solution)/shard_map/all_to_all | solution.py:43
  94.5 145.4 %all-gather.4.cloned.1.call-start = ((), (), s32[]{:S(2)}) async-start(), calls=%async_computation.8 | async-start | bytes 4718592 | tf_op jit(solution)/shard_map/all_gather | solution.py:72
  95.7 287.6 %all-reduce.3.cloned.1.call-start = ((), (), s32[]{:S(2)}) async-start(), calls=%async_computation.14 | async-start | bytes 131072
  286.7 181.4 %reduce-scatter.4.cloned.1.call-start = ((), (), s32[]{:S(2)}) async-start(), calls=%async_computation.9 | async-start | bytes 4456448 | tf_op jit(solution)/shard_map/reduce_scatter | solution.py:79
  365.1 8.7 copy-start.5
  373.7 222.2 %all-gather.6.cloned.1.call-start = ((), (), s32[]{:S(2)}) async-start(), calls=%async_computation.10 | async-start | bytes 4718592 | tf_op jit(solution)/shard_map/all_gather | solution.py:72
  567.1 224.7 %reduce-scatter.6.cloned.1.call-start = ((), (), s32[]{:S(2)}) async-start(), calls=%async_computation.11 | async-start | bytes 4456448 | tf_op jit(solution)/shard_map/reduce_scatter | solution.py:79
  613.7 14.4 %copy-start.1 = (bf16[64,128,128]{2,1,0:T(8,128)(2,1)S(1)}, bf16[64,128,128]{2,1,0:T(8,128)(2,1)}, u32[]{:S(2)}) copy-start(bf16[64,128,128]{2,1,0:T(8,128)(2,1)} %param.11) | copy-start | bytes 6291460
  715.8 203.9 %all-gather.8.cloned.1.call-start = ((), (), s32[]{:S(2)}) async-start(), calls=%async_computation.12 | async-start | bytes 4718592 | tf_op jit(solution)/shard_map/all_gather | solution.py:72
  890.8 223.4 %reduce-scatter.8.cloned.1.call-start = ((), (), s32[]{:S(2)}) async-start(), calls=%async_computation.13 | async-start | bytes 4456448 | tf_op jit(solution)/shard_map/reduce_scatter | solution.py:79
  937.5 14.4 %copy-start.2 = (bf16[64,128,128]{2,1,0:T(8,128)(2,1)S(1)}, bf16[64,128,128]{2,1,0:T(8,128)(2,1)}, u32[]{:S(2)}) copy-start(bf16[64,128,128]{2,1,0:T(8,128)(2,1)} %param.11) | copy-start | bytes 6291460
Sparse Core Ops, SparseCore 0:
  97.1 142.6 all-gather.3
  567.2 28.7 all-gather.5
  891.0 28.7 all-gather.7
Sparse Core Ops, SparseCore 1:
  286.7 96.5 all-reduce.2
  386.9 81.1 reduce-scatter.3
  715.9 75.8 reduce-scatter.5
  1038.8 75.4 reduce-scatter.7
where the time goes:
time: 1210 us; the launch traced here: 1200 us
  waiting for transfers between devices  451 us (37%)
  other arithmetic  283 us (23%)
  blocking collectives  230 us (19%)
  local copies, waits for them, and re-layouts  137 us (11%)
  matrix products  59.8 us (5%)
  starting transfers between devices  26.3 us (2%)
  between operations  16.4 us (1%)
    reduce_scatter x3, waiting for transfers between devices, local(): lax.psum_scatter(partial_value.reshape(row_blocks * tile_size, feature_wi...  235 us
    all_gather x3, waiting for transfers between devices, local(): lax.all_gather(received_terms.reshape(rows_dev, feature_width), 'row', ax...  200 us
    psum x3, blocking collectives, local(): gram = lax.psum(local_gram, ('row', 'col')) / nodes  199 us
    scatter-add x3, other arithmetic, block_terms(): jax.ops.segment_sum(taken_terms, taken_rows, row_blocks)  179 us
    dot_general x3, matrix products, block_terms(): jnp.einsum('nab,nak->nbk', taken, blocked[taken_cols], preferred_element_...  43.1 us
    gather x3, local copies, waits for them, and re-layouts, block_terms(): blocked[taken_cols]  39.8 us
    all_to_all x2, blocking collectives, local(): lax.all_to_all(current.reshape(devices, sub_rows, feature_width), ('row',...  31.5 us
    scatter x1, local copies, waits for them, and re-layouts, local(): outgoing = jnp.zeros((devices, CAP, tile_size, tile_size), jnp.bfloat16)....  30.8 us
  transfers between devices with their start and end apart: 10, of which 8 were waited for; matrix products, arithmetic and copies ran while one was open for 14% of the time, Pallas kernels for 0%

commit v1 on v0

--- a/solution.py
+++ b/solution.py
@@ -86,7 +86,7 @@
         local_gram = jnp.dot(
             scaled.T, scaled, precision=lax.Precision.HIGHEST, preferred_element_type=jnp.float32
         )
-        gram = lax.psum(local_gram, ("row", "col")) / nodes
+        gram = lax.psum(lax.psum(local_gram, "row"), "col") / nodes
         lower = jnp.linalg.cholesky(gram)
         final_output = lax.linalg.triangular_solve(
             lower, scaled, left_side=False, lower=True, transpose_a=True

time: 1210 us -> 1310 us (1.083); the launches traced: 1200 us -> 1280 us
  blocking collectives: 230 us -> 306 us
    psum x3 -> x6, blocking collectives: 199 us -> 243 us  [local(): gram = lax.psum(lax.psum(local_gram, 'row'), 'col') / nodes]
    all_to_all x2, blocking collectives: 31.5 us -> 62.9 us  [local(): lax.all_to_all(current.reshape(devices, sub_rows, feature_width), ('row',...]
  transfers between devices with their start and end apart: 10 -> 10, of which waited for: 8 -> 8; matrix products, arithmetic and copies ran while one was open for 14% -> 13% of each run, Pallas kernels for 0% -> 0%
where the time goes in v1:
time: 1310 us; the launch traced here: 1280 us
  waiting for transfers between devices  452 us (35%)
  blocking collectives  306 us (23%)
  other arithmetic  283 us (22%)
  local copies, waits for them, and re-layouts  137 us (10%)
  matrix products  59.8 us (5%)
  starting transfers between devices  26.2 us (2%)
  between operations  16.4 us (1%)
    psum x6, blocking collectives, local(): gram = lax.psum(lax.psum(local_gram, 'row'), 'col') / nodes  243 us
    reduce_scatter x3, waiting for transfers between devices, local(): lax.psum_scatter(partial_value.reshape(row_blocks * tile_size, feature_wi...  235 us
    all_gather x3, waiting for transfers between devices, local(): lax.all_gather(received_terms.reshape(rows_dev, feature_width), 'row', ax...  200 us
    scatter-add x3, other arithmetic, block_terms(): jax.ops.segment_sum(taken_terms, taken_rows, row_blocks)  179 us
    all_to_all x2, blocking collectives, local(): lax.all_to_all(current.reshape(devices, sub_rows, feature_width), ('row',...  62.9 us
    dot_general x3, matrix products, block_terms(): jnp.einsum('nab,nak->nbk', taken, blocked[taken_cols], preferred_element_...  43.1 us
    gather x3, local copies, waits for them, and re-layouts, block_terms(): blocked[taken_cols]  39.8 us
    scatter x1, local copies, waits for them, and re-layouts, local(): outgoing = jnp.zeros((devices, CAP, tile_size, tile_size), jnp.bfloat16)....  30.8 us
  transfers between devices with their start and end apart: 10, of which 8 were waited for; matrix products, arithmetic and copies ran while one was open for 13% of the time, Pallas kernels for 0%

profile of v1, /device:TPU:1, one launch (start us, length us, event | category | flops | bytes accessed | tf_op | source)
XLA Modules:
  0.0 1281.0 jit_solution(10334512079006830600)
XLA Ops:
  8.4 10.1 scatter_fusion.1
  20.0 11.5 all-to-all-start.1
  33.8 7.8 all-to-all-done.1
  45.7 7.7 broadcast_in_dim.14
  53.4 30.8 %scatter_fusion.2 = bf16[128,3,128,128]{3,2,1,0:T(8,128)(2,1)} fusion(bf16[128,3,128,128]{3,2,1,0:T(8,128)(2,1)} %broadcast_in_dim.14, s32[192]{0:T(256)S(1)} %bitcast.91, bf16[192,128,128]{2,1,0:T(8,128)(2,1)} %param.14), kind=kCustom, calls=%fused_computation.8 | custom fusion | bytes 18875904 | tf_op jit(solution)/shard_map/scatter | solution.py:38
  84.2 10.2 all-to-all-start.2
  97.6 142.3 %all-gather.4.cloned.1.call-done = bf16[16384,64]{1,0:T(8,128)(2,1)} async-done(((bf16[2048,64]{1,0:T(8,128)(2,1)}), bf16[16384,64]{1,0:T(8,128)(2,1)}) %all-gather.4.cloned.1.call-update) | async-done | bytes 2097168 | tf_op jit(solution)/shard_map/all_gather | solution.py:72
  243.8 13.3 %gather_fusion.1 = bf16[384,128,64]{1,2,0:T(8,128)(2,1)} fusion(bf16[128,128,64]{1,2,0:T(8,128)(2,1)S(1)} %copy.77, s32[1024]{0:T(1024)S(1)} %pad_clamp_fusion), kind=kCustom, calls=%fused_computation.1 | custom fusion | bytes 12584448 | tf_op jit(solution)/shard_map/gather | solution.py:15
  260.9 4.3 broadcast.110.clone.2
  265.2 9.0 scatter_fusion
  274.2 9.2 convert_reduce_fusion
  286.7 14.3 %fusion.38 = f32[384,128,64]{1,2,0:T(8,128)} fusion(bf16[384,128,64]{1,2,0:T(8,128)(2,1)} %gather_fusion.1, bf16[384,128,128]{2,1,0:T(8,128)(2,1)} %bitcast.9), kind=kOutput, calls=%fused_computation.120 | convolution fusion | flops 805306368 | bytes 31457280 | tf_op jit(solution)/shard_map/nab,nak->nbk/dot_general | solution.py:14
  301.0 4.3 broadcast.110.clone.3
  305.3 59.8 %scatter_fusion.3 = f32[256,128,64]{1,2,0:T(8,128)} fusion(f32[256,128,64]{1,2,0:T(8,128)} %broadcast.110.clone.3, s32[384]{0:T(512)S(1)} %get-tuple-element.8, f32[384,128,64]{1,2,0:T(8,128)} %fusion.38), kind=kCustom, calls=%fused_computation.9 | custom fusion | flops 3145728 | bytes 37750272 | tf_op jit(solution)/shard_map/scatter-add | solution.py:17
  365.1 8.6 copy_bitcast_fusion.2
  375.0 8.3 all-reduce.3.cloned.1.call-done
  384.0 84.0 %reduce-scatter.4.cloned.1.call-done = bf16[2048,64]{0,1:T(8,128)(2,1)} async-done(((bf16[32768,64]{0,1:T(8,128)(2,1)}), bf16[2048,64]{0,1:T(8,128)(2,1)}) %reduce-scatter.4.cloned.1.call-update) | async-done | bytes 262160 | tf_op jit(solution)/shard_map/reduce_scatter | solution.py:79
  469.7 22.9 %psum.42 = f32[64,64]{0,1:T(8,128)S(1)} all-reduce(f32[64,64]{0,1:T(8,128)S(1)} %fusion.5), channel_id=1, replica_groups=mesh['row'=8,'col'=16] {'row'}, use_global_device_ids=true, to_apply=%region_11.12 | all-reduce | flops 4096 | bytes 32768 | tf_op jit(solution)/shard_map/psum | solution.py:89
  492.6 58.2 %psum.43 = f32[64,64]{0,1:T(8,128)S(1)} all-reduce(f32[64,64]{0,1:T(8,128)S(1)} %psum.42), channel_id=1, replica_groups=mesh['row'=8,'col'=16] {'col'}, use_global_device_ids=true, to_apply=%region_12.13 | all-reduce | flops 4096 | bytes 32768 | tf_op jit(solution)/shard_map/psum | solution.py:89
  550.9 5.8 cholesky.59
  558.1 4.9 custom-call.11
  565.2 31.5 %all_to_all.25 = bf16[128,2,512]{2,1,0:T(2,128)(2,1)S(1)} all-to-all(bf16[128,2,512]{2,1,0:T(2,128)(2,1)S(1)} %reshape.237), channel_id=1, replica_groups=mesh['row'=8,'col'=16] {'row','col'}, dimensions={0} | all-to-all | bytes 524288 | tf_op jit(solution)/shard_map/all_to_all | solution.py:65
  597.9 28.8 %all-gather.6.cloned.1.call-done = bf16[16384,64]{1,0:T(8,128)(2,1)} async-done(((bf16[2048,64]{1,0:T(8,128)(2,1)}), bf16[16384,64]{1,0:T(8,128)(2,1)}) %all-gather.6.cloned.1.call-update) | async-done | bytes 2097168 | tf_op jit(solution)/shard_map/all_gather | solution.py:72
  630.5 13.3 %gather_fusion.3 = bf16[384,128,64]{1,2,0:T(8,128)(2,1)} fusion(bf16[128,128,64]{1,2,0:T(8,128)(2,1)S(1)} %copy.87, s32[1024]{0:T(1024)S(1)} %pad_clamp_fusion), kind=kCustom, calls=%fused_computation.3 | custom fusion | bytes 12584448 | tf_op jit(solution)/shard_map/gather | solution.py:15
  644.6 14.4 %fusion.39 = f32[384,128,64]{1,2,0:T(8,128)} fusion(bf16[384,128,64]{1,2,0:T(8,128)(2,1)} %gather_fusion.3, bf16[384,128,128]{2,1,0:T(8,128)(2,1)} %bitcast.9), kind=kOutput, calls=%fused_computation.121 | convolution fusion | flops 805306368 | bytes 31457280 | tf_op jit(solution)/shard_map/nab,nak->nbk/dot_general | solution.py:14
  660.5 4.3 broadcast.110.clone.4
  664.8 59.8 %scatter_fusion.5 = f32[256,128,64]{1,2,0:T(8,128)} fusion(f32[256,128,64]{1,2,0:T(8,128)} %broadcast.110.clone.4, s32[384]{0:T(512)S(1)} %get-tuple-element.8, f32[384,128,64]{1,2,0:T(8,128)} %fusion.39), kind=kCustom, calls=%fused_computation.13 | custom fusion | flops 3145728 | bytes 37750272 | tf_op jit(solution)/shard_map/scatter-add | solution.py:17
  728.9 9.2 scatter_fusion.4
  738.1 8.6 copy_bitcast_fusion.1
  746.8 75.9 %reduce-scatter.6.cloned.1.call-done = bf16[2048,64]{0,1:T(8,128)(2,1)} async-done(((bf16[32768,64]{0,1:T(8,128)(2,1)}), bf16[2048,64]{0,1:T(8,128)(2,1)}) %reduce-scatter.6.cloned.1.call-update) | async-done | bytes 262160 | tf_op jit(solution)/shard_map/reduce_scatter | solution.py:79
  824.3 22.9 %psum.44 = f32[64,64]{0,1:T(8,128)S(1)} all-reduce(f32[64,64]{0,1:T(8,128)S(1)} %fusion.6), channel_id=1, replica_groups=mesh['row'=8,'col'=16] {'row'}, use_global_device_ids=true, to_apply=%region_18.21 | all-reduce | flops 4096 | bytes 32768 | tf_op jit(solution)/shard_map/psum | solution.py:89
  847.3 58.2 %psum.45 = f32[64,64]{0,1:T(8,128)S(1)} all-reduce(f32[64,64]{0,1:T(8,128)S(1)} %psum.44), channel_id=1, replica_groups=mesh['row'=8,'col'=16] {'col'}, use_global_device_ids=true, to_apply=%region_19.22 | all-reduce | flops 4096 | bytes 32768 | tf_op jit(solution)/shard_map/psum | solution.py:89
  905.5 5.8 cholesky.70
  912.7 4.9 custom-call.12
  919.8 31.5 %all_to_all.26 = bf16[128,2,512]{2,1,0:T(2,128)(2,1)S(1)} all-to-all(bf16[128,2,512]{2,1,0:T(2,128)(2,1)S(1)} %reshape.239), channel_id=1, replica_groups=mesh['row'=8,'col'=16] {'row','col'}, dimensions={0} | all-to-all | bytes 524288 | tf_op jit(solution)/shard_map/all_to_all | solution.py:65
  952.5 28.8 %all-gather.8.cloned.1.call-done = bf16[16384,64]{1,0:T(8,128)(2,1)} async-done(((bf16[2048,64]{1,0:T(8,128)(2,1)}), bf16[16384,64]{1,0:T(8,128)(2,1)}) %all-gather.8.cloned.1.call-update) | async-done | bytes 2097168 | tf_op jit(solution)/shard_map/all_gather | solution.py:72
  985.0 13.3 %gather_fusion.5 = bf16[384,128,64]{1,2,0:T(8,128)(2,1)} fusion(bf16[128,128,64]{1,2,0:T(8,128)(2,1)S(1)} %copy.94, s32[1024]{0:T(1024)S(1)} %pad_clamp_fusion), kind=kCustom, calls=%fused_computation.5 | custom fusion | bytes 12584448 | tf_op jit(solution)/shard_map/gather | solution.py:15
  999.0 14.4 %fusion.40 = f32[384,128,64]{1,2,0:T(8,128)} fusion(bf16[384,128,64]{1,2,0:T(8,128)(2,1)} %gather_fusion.5, bf16[384,128,128]{2,1,0:T(8,128)(2,1)} %bitcast.9), kind=kOutput, calls=%fused_computation.122 | convolution fusion | flops 805306368 | bytes 31457280 | tf_op jit(solution)/shard_map/nab,nak->nbk/dot_general | solution.py:14
  1015.0 4.3 broadcast.110.clone.5
  1019.3 58.9 %scatter_fusion.7 = f32[256,128,64]{1,2,0:T(8,128)} fusion(f32[256,128,64]{1,2,0:T(8,128)} %broadcast.110.clone.5, s32[384]{0:T(512)S(1)} %get-tuple-element.8, f32[384,128,64]{1,2,0:T(8,128)} %fusion.40), kind=kCustom, calls=%fused_computation.15 | custom fusion | flops 3145728 | bytes 37750272 | tf_op jit(solution)/shard_map/scatter-add | solution.py:17
  1078.2 4.3 broadcast.110.clone
  1082.5 9.2 scatter_fusion.6
  1091.7 8.5 copy_bitcast_fusion
  1100.3 75.5 %reduce-scatter.8.cloned.1.call-done = bf16[2048,64]{0,1:T(8,128)(2,1)} async-done(((bf16[32768,64]{0,1:T(8,128)(2,1)}), bf16[2048,64]{0,1:T(8,128)(2,1)}) %reduce-scatter.8.cloned.1.call-update) | async-done | bytes 262160 | tf_op jit(solution)/shard_map/reduce_scatter | solution.py:79
  1177.4 23.0 %psum.46 = f32[64,64]{0,1:T(8,128)S(1)} all-reduce(f32[64,64]{0,1:T(8,128)S(1)} %fusion.7), channel_id=1, replica_groups=mesh['row'=8,'col'=16] {'row'}, use_global_device_ids=true, to_apply=%region_23.26 | all-reduce | flops 4096 | bytes 32768 | tf_op jit(solution)/shard_map/psum | solution.py:89
  1200.4 58.2 %psum.47 = f32[64,64]{0,1:T(8,128)S(1)} all-reduce(f32[64,64]{0,1:T(8,128)S(1)} %psum.46), channel_id=1, replica_groups=mesh['row'=8,'col'=16] {'col'}, use_global_device_ids=true, to_apply=%region_24.27 | all-reduce | flops 4096 | bytes 32768 | tf_op jit(solution)/shard_map/psum | solution.py:89
  1258.7 5.8 cholesky.81
  1265.9 4.9 custom-call.13
  (93 shorter events, 59.0 us)
Async XLA Ops:
  20.0 21.6 %all-to-all-start.1 = ((s32[128,3,2]{1,2,0:T(2,128)}), s32[128,3,2]{1,2,0:T(2,128)S(1)}, u32[]{:S(2)}, u32[]{:S(2)}) async-start(s32[128,3,2]{1,2,0:T(2,128)} %copy.79), calls=%async_computation.1 | async-start | bytes 262144 | tf_op jit(solution)/shard_map/all_to_all | solution.py:44
  41.6 42.6 %all-to-all-start = ((bf16[128,2,512]{2,1,0:T(2,128)(2,1)}), bf16[128,2,512]{2,1,0:T(2,128)(2,1)S(1)}, u32[]{:S(2)}, u32[]{:S(2)}) async-start(bf16[128,2,512]{2,1,0:T(2,128)(2,1)} %reshape.235), calls=%async_computation | async-start | bytes 524288 | tf_op jit(solution)/shard_map/all_to_all | solution.py:65
  84.2 11.5 copy-start.3
  84.2 11.6 copy-start
  84.2 13.1 %copy-start.4 = (s32[64]{0:T(128)S(1)}, s32[64]{0:T(128)}, u32[]{:S(2)}) copy-start(s32[64]{0:T(128)} %param.13) | copy-start | bytes 772
  84.2 190.0 %all-to-all-start.2 = ((bf16[128,3,128,128]{3,2,1,0:T(8,128)(2,1)}), bf16[128,3,128,128]{3,2,1,0:T(8,128)(2,1)}, u32[]{:S(2)}, u32[]{:S(2)}) async-start(bf16[128,3,128,128]{3,2,1,0:T(8,128)(2,1)} %scatter_fusion.2), calls=%async_computation.2 | async-start | bytes 25165824 | tf_op jit(solution)/shard_map/all_to_all | solution.py:43
  94.5 145.4 %all-gather.4.cloned.1.call-start = ((), (), s32[]{:S(2)}) async-start(), calls=%async_computation.8 | async-start | bytes 4718592 | tf_op jit(solution)/shard_map/all_gather | solution.py:72
  95.7 287.6 %all-reduce.3.cloned.1.call-start = ((), (), s32[]{:S(2)}) async-start(), calls=%async_computation.14 | async-start | bytes 131072
  286.7 181.4 %reduce-scatter.4.cloned.1.call-start = ((), (), s32[]{:S(2)}) async-start(), calls=%async_computation.9 | async-start | bytes 4456448 | tf_op jit(solution)/shard_map/reduce_scatter | solution.py:79
  365.1 8.7 copy-start.5
  373.7 253.0 %all-gather.6.cloned.1.call-start = ((), (), s32[]{:S(2)}) async-start(), calls=%async_computation.10 | async-start | bytes 4718592 | tf_op jit(solution)/shard_map/all_gather | solution.py:72
  597.8 224.9 %reduce-scatter.6.cloned.1.call-start = ((), (), s32[]{:S(2)}) async-start(), calls=%async_computation.11 | async-start | bytes 4456448 | tf_op jit(solution)/shard_map/reduce_scatter | solution.py:79
  644.6 14.4 %copy-start.1 = (bf16[64,128,128]{2,1,0:T(8,128)(2,1)S(1)}, bf16[64,128,128]{2,1,0:T(8,128)(2,1)}, u32[]{:S(2)}) copy-start(bf16[64,128,128]{2,1,0:T(8,128)(2,1)} %param.11) | copy-start | bytes 6291460
  746.7 234.6 %all-gather.8.cloned.1.call-start = ((), (), s32[]{:S(2)}) async-start(), calls=%async_computation.12 | async-start | bytes 4718592 | tf_op jit(solution)/shard_map/all_gather | solution.py:72
  952.4 223.4 %reduce-scatter.8.cloned.1.call-start = ((), (), s32[]{:S(2)}) async-start(), calls=%async_computation.13 | async-start | bytes 4456448 | tf_op jit(solution)/shard_map/reduce_scatter | solution.py:79
  999.0 14.4 %copy-start.2 = (bf16[64,128,128]{2,1,0:T(8,128)(2,1)S(1)}, bf16[64,128,128]{2,1,0:T(8,128)(2,1)}, u32[]{:S(2)}) copy-start(bf16[64,128,128]{2,1,0:T(8,128)(2,1)} %param.11) | copy-start | bytes 6291460
Sparse Core Ops, SparseCore 0:
  97.1 142.6 all-gather.3
  597.9 28.7 all-gather.5
  952.5 28.7 all-gather.7
Sparse Core Ops, SparseCore 1:
  286.7 96.5 all-reduce.2
  386.9 81.1 reduce-scatter.3
  746.8 75.8 reduce-scatter.5
  1100.3 75.4 reduce-scatter.7
